TPU v7x, 128 devices: a whole 4x4x4 slice. The times are simulated.
128 devices in a mesh: rows: 16 (over x, y), cols: 8 (over z, core).
Axes of the slice: x: 4, y: 4, z: 4, core: 2. Of those that a mesh axis runs over, the one named last changes fastest.
Arguments:
- affinity: bfloat16 [8, 128, 8, 8, 4096], P(None, 'rows', 'cols'), may hold values from -6 to 6
- block_columns: int32 [8, 128, 8, 8], P(None, 'rows', 'cols'), may hold values from 0 to 127
- block_counts: int32 [8, 128, 8], P(None, 'rows', 'cols'), may hold values from 0 to 8
- inv_degree: float32 [8, 128, 64], P('cols', 'rows'), may hold values from 0.4 to 6.1
- panel: float32 [8, 128, 4096], P('cols', 'rows'), may hold values from -6 to 6
Outputs:
- panel_out: float32 [8, 128, 4096], P('cols', 'rows')
Inputs may be any that keep to these rules, and one draw needn't show every extreme that they name: `block_columns`: slots at or past a block row's count are ignored; listed block columns may repeat, and their blocks then add.
All inputs are finite; a program needn't handle non-finite values.
Results may differ from a plain program's by a relative error of at most 0.019.
Values may be sent and summed in bfloat16 or wider, within the bound.
A program may use at most 128 MiB of HBM per device.

v0:
```python
import functools

import jax
import jax.numpy as jnp
from jax import lax
from jax.experimental import pallas as pl
from jax.experimental.pallas import tpu as pltpu
from jax.sharding import PartitionSpec as P

ITERS = 2
SIDE = 4
B = 64
G = 8
R = 8
S = 8
H = B // 2
LANES = 128
NB = 128
MESH = pl.DeviceIdType.MESH
HIGHEST = lax.Precision.HIGHEST
F32 = jnp.float32
BF16 = jnp.bfloat16


def low_lanes(rows):
    return lax.broadcasted_iota(jnp.int32, (rows, LANES), 1) < B


def trade(u, v, low):
    crossed = pltpu.roll(jnp.where(low, v, u), B, 1)
    return jnp.where(low, u, crossed), jnp.where(low, crossed, v)


def inverse_factor(gram):
    row = lax.broadcasted_iota(jnp.int32, (B, LANES), 0)
    lane = lax.broadcasted_iota(jnp.int32, (B, LANES), 1)
    m = jnp.where(lane < B, gram, jnp.where(lane - B == row, 1.0, 0.0).astype(F32))
    done = []
    for block in range(B // 8):
        height = B - 8 * block
        rows = lax.broadcasted_iota(jnp.int32, (height, LANES), 0)
        columns = [
            jnp.broadcast_to(m[:, 8 * block + j : 8 * block + j + 1], (height, LANES))
            for j in range(8)
        ]
        for j in range(8):
            ratio = columns[j] * (1.0 / columns[j][j : j + 1, :])
            ratio = jnp.where(rows > j, ratio, 0.0)
            for later in range(j + 1, 8):
                columns[later] = columns[later] - ratio * columns[later][j : j + 1, :]
            m = m - ratio * m[j : j + 1, :]
        done.append(m[:8])
        m = m[8:]
    m = jnp.concatenate(done, axis=0)
    pivots = jnp.sum(jnp.where(lane == row, m, 0.0), axis=1, keepdims=True)
    return m * lax.rsqrt(pivots)


def twice(inverse):
    low = low_lanes(B)
    upper = jnp.where(low, pltpu.roll(inverse, B, 1), 0.0)
    lower = jnp.where(low, 0.0, inverse)
    return jnp.concatenate([upper, lower], axis=0)


def times_transpose(rows, factor):
    return lax.dot_general(
        rows, factor, (((1,), (1,)), ((), ())), precision=HIGHEST, preferred_element_type=F32
    )


def kernel(
    total_rows,
    columns_ref, counts_ref, affinity_ref, inverse_ref, panel_ref,
    out_ref,
    raw, blocks, stage, degree, rows_ref, pack, gathered, table, outgoing, incoming,
    gram_z, gram_x, gram_y,
    raw_sem, ag_send, ag_recv, rs_send, rs_recv, gz_send, gz_recv, gx_send, gx_recv, gy_send, gy_recv,
):
    mine_r, mine_c = lax.axis_index("rows"), lax.axis_index("cols")
    x, y = mine_r // SIDE, lax.rem(mine_r, SIDE)
    z, core = mine_c // 2, lax.rem(mine_c, 2)

    def row_of(dx, dy):
        return lax.rem(x + dx + SIDE, SIDE) * SIDE + lax.rem(y + dy + SIDE, SIDE)

    def col_of(dz, dc):
        return lax.rem(z + dz, SIDE) * 2 + lax.rem(core + dc, 2)

    x_peers = [row_of(d, 0) for d in (1, 2, 3)]
    y_peers = [row_of(0, d) for d in (1, 2, 3)]
    order = [(2, 0), (2, 1), (1, 0), (3, 0), (1, 1), (3, 1), (0, 1)]
    z_peers = [col_of(*d) for d in order]

    for g in range(G):
        pltpu.make_async_copy(affinity_ref.at[g], raw.at[g], raw_sem.at[g]).start()

    barrier = pltpu.get_barrier_semaphore()
    for peer in x_peers + y_peers:
        pl.semaphore_signal(barrier, inc=1, device_id={"rows": peer}, device_id_type=MESH)
    for peer in z_peers:
        pl.semaphore_signal(barrier, inc=1, device_id={"cols": peer}, device_id_type=MESH)

    spread = lax.broadcasted_iota(jnp.int32, (H, B), 1) // 2 == lax.broadcasted_iota(jnp.int32, (H, B), 0)
    picked = jnp.concatenate(
        [jnp.where(spread, jnp.broadcast_to(inverse_ref[i : i + 1, :], (H, B)), 0.0) for i in range(R)], axis=0
    )
    halves = (
        lax.rem(lax.broadcasted_iota(jnp.int32, (B, LANES), 0), 2)
        == lax.broadcasted_iota(jnp.int32, (B, LANES), 1) // B
    )
    degree[...] = jnp.dot(
        picked, jnp.where(halves, 1.0, 0.0).astype(F32), precision=HIGHEST, preferred_element_type=F32
    )
    for t in range(H):
        rows_ref[pl.ds(t, R, stride=H), :] = panel_ref[:, t * LANES : (t + 1) * LANES]

    low_h = low_lanes(H)
    low_b = low_lanes(B)

    def fill_own(it):
        for pair in range(4):
            rows = slice(2 * pair * H, 2 * pair * H + B)
            scaled = rows_ref[rows, :] * degree[rows, :]
            even, odd = trade(scaled[:H], scaled[H:], low_h)
            pack[pl.ds(pair * B, H, stride=2), :] = even
            pack[pl.ds(pair * B + 1, H, stride=2), :] = odd
            gathered[it, mine_r * 4 + pair] = pack[pair * B : (pair + 1) * B, :].astype(BF16)

    def ag_copy(it, slot, number, peer):
        return pltpu.make_async_remote_copy(
            src_ref=gathered.at[it, slot],
            dst_ref=gathered.at[it, slot],
            send_sem=ag_send.at[it, number],
            recv_sem=ag_recv.at[it, slot],
            device_id={"rows": peer},
            device_id_type=MESH,
        )

    pending = []

    def expand(it, slot):
        pair = gathered[it, slot]
        zero = jnp.zeros_like(pair)
        table[2 * slot] = jnp.where(low_b, pair, zero)
        table[2 * slot + 1] = jnp.where(low_b, zero, pair)

    def all_gather(it, meanwhile):
        sent = [0]
        px, nx, py, ny = row_of(1, 0), row_of(-1, 0), row_of(0, 1), row_of(0, -1)

        def slot_of(dx, dy, pair):
            return row_of(dx, dy) * 4 + pair

        def send(dx, dy, pair, peer):
            copy = ag_copy(it, slot_of(dx, dy, pair), sent[0], peer)
            sent[0] += 1
            copy.start()
            pending.append(copy)

        def take(dx, dy, pair, *peers):
            slot = slot_of(dx, dy, pair)
            ag_copy(it, slot, 0, mine_r).wait_recv()
            for peer in peers:
                send(dx, dy, pair, peer)
            expand(it, slot)

        for peers_a, peers_b in (((px, nx), (py, ny)), ((py, ny), (px, nx))):
            for number in range(2):
                for peer_a, peer_b in zip(peers_a, peers_b):
                    send(0, 0, number, peer_a)
                    send(0, 0, 2 + number, peer_b)
        for pair in range(4):
            expand(it, slot_of(0, 0, pair))
        meanwhile(0)
        take(-1, 0, 0, px, py, ny)
        take(1, 0, 1, nx, py, ny)
        take(0, -1, 2, py, px, nx)
        take(0, 1, 3, ny, px, nx)
        take(-1, 0, 1, py, ny)
        take(1, 0, 0, py, ny)
        take(0, -1, 3, px, nx)
        take(0, 1, 2, px, nx)
        meanwhile(1)
        take(0, -1, 0, py)
        take(0, 1, 1, ny)
        take(-1, 0, 2, px)
        take(1, 0, 3, nx)
        meanwhile(2)
        take(2, 0, 0, py, ny)
        take(2, 0, 1, py, ny)
        take(0, 2, 2, px, nx)
        take(0, 2, 3, px, nx)
        meanwhile(3)
        for d in (-1, 1):
            take(d, -1, 0, py)
            take(d, 1, 1, ny)
            take(-1, d, 2, px)
            take(1, d, 3, nx)
        meanwhile(4)
        take(2, -1, 0, py)
        take(2, 1, 1, ny)
        take(-1, 2, 2, px)
        take(1, 2, 3, nx)
        meanwhile(5)
        for d in (0, -1, 1, 2):
            if d == 0:
                take(0, -1, 1)
                take(0, 1, 0)
                take(-1, 0, 3)
                take(1, 0, 2)
            else:
                take(d, -1, 1)
                take(d, 1, 0)
                take(-1, d, 3)
                take(1, d, 2)
            take(d, 2, 0)
            take(d, 2, 1)
            take(2, d, 2)
            take(2, d, 3)

    def arrange(g):
        pltpu.make_async_copy(affinity_ref.at[g], raw.at[g], raw_sem.at[g]).wait()

        def one(i, carry):
            for t in range(H):
                stage[pl.ds(t, S, stride=H), :] = raw[g, i, :, t * LANES : (t + 1) * LANES].astype(F32)
            for u in range(S // 2):
                upper, lower = trade(
                    stage[2 * u * H : (2 * u + 1) * H, :], stage[(2 * u + 1) * H : (2 * u + 2) * H, :], low_h
                )
                blocks[g * R + i, 0:H, u * LANES : (u + 1) * LANES] = upper.astype(BF16)
                blocks[g * R + i, H:B, u * LANES : (u + 1) * LANES] = lower.astype(BF16)
            return carry

        lax.fori_loop(0, R, one, 0)

    def product(g, i):
        count = counts_ref[g, i]
        right = []
        for s in range(S):
            column = jnp.where(s < count, columns_ref[g, i, s], NB)
            right.append(table[column])
        o = jnp.dot(blocks[g * R + i], jnp.concatenate(right, axis=0), preferred_element_type=F32)
        even, odd = o[:H], o[H:]
        return jnp.where(low_h, even, odd) + pltpu.roll(jnp.where(low_h, odd, even), B, 1)

    def rs_copy(it, k, peer):
        return pltpu.make_async_remote_copy(
            src_ref=outgoing.at[it, k],
            dst_ref=incoming.at[it, mine_c],
            send_sem=rs_send.at[it, k],
            recv_sem=rs_recv.at[it, mine_c],
            device_id={"cols": peer},
            device_id_type=MESH,
        )

    UNROLL = 4

    def multiply(it):
        for k, peer in enumerate(z_peers + [mine_c]):
            def some(step, carry):
                for j in range(UNROLL):
                    i = step * UNROLL + j
                    term = product(peer, i).astype(BF16)
                    at = pl.ds(pl.multiple_of(i * H, H), H)
                    if k < G - 1:
                        outgoing[it, k, at, :] = term
                    else:
                        incoming[it, mine_c, at, :] = term
                return carry

            lax.fori_loop(0, R // UNROLL, some, 0)
            if k < G - 1:
                copy = rs_copy(it, k, peer)
                copy.start()
                pending.append(copy)

    def collect(it):
        for peer in reversed(z_peers):
            pltpu.make_async_remote_copy(
                src_ref=outgoing.at[it, 0],
                dst_ref=incoming.at[it, peer],
                send_sem=rs_send.at[it, 0],
                recv_sem=rs_recv.at[it, peer],
                device_id={"cols": peer},
                device_id_type=MESH,
            ).wait_recv()
        summed = incoming[it, 0].astype(F32)
        for c in range(1, G):
            summed = summed + incoming[it, c].astype(F32)
        return summed * degree[...]

    def exchange(it, buffer, send_sem, recv_sem, at, axis, peers, slots):
        def copy(n, slot):
            return pltpu.make_async_remote_copy(
                src_ref=buffer.at[it, at],
                dst_ref=buffer.at[it, slot],
                send_sem=send_sem.at[it, n],
                recv_sem=recv_sem.at[it, slot],
                device_id={axis: peers[n]},
                device_id_type=MESH,
            )

        def start():
            for n in range(len(peers)):
                c = copy(n, at)
                c.start()
                pending.append(c)

        def finish():
            for n in range(len(peers)):
                copy(n, slots[n]).wait_recv()
            total = buffer[it, 0]
            for n in range(1, len(peers) + 1):
                total = total + buffer[it, n]
            return total

        return start, finish

    def gram_of(it):
        along_z = exchange(it, gram_z, gz_send, gz_recv, mine_c, "cols", z_peers, z_peers)
        along_x = exchange(it, gram_x, gx_send, gx_recv, x, "rows", x_peers, [p // SIDE for p in x_peers])
        along_y = exchange(it, gram_y, gy_send, gy_recv, y, "rows", y_peers, [lax.rem(p, SIDE) for p in y_peers])

        def first():
            rows = rows_ref[...]
            both = lax.dot_general(
                rows, rows, (((0,), (0,)), ((), ())), precision=HIGHEST, preferred_element_type=F32
            )
            gram = both[:B] + pltpu.roll(both[B:], B, 1)
            gram_z[it, mine_c] = jnp.where(low_h, gram[:H], pltpu.roll(gram[H:], B, 1))
            along_z[0]()

        def second():
            gram_x[it, x] = along_z[1]()
            along_x[0]()

        def third():
            gram_y[it, y] = along_x[1]()
            along_y[0]()

        def last():
            total = along_y[1]() * (1.0 / total_rows)
            return jnp.concatenate([total, pltpu.roll(total, B, 1)], axis=0)

        return first, second, third, last

    fill_own(0)
    table[NB] = jnp.zeros((B, LANES), BF16)
    pl.semaphore_wait(barrier, len(x_peers) + len(y_peers) + len(z_peers))

    shares = [(0, 1), (2,), (3,), (4, 5), (6,), (7,)]

    def arranging(n):
        for g in shares[n]:
            arrange(g)

    all_gather(0, arranging)
    multiply(0)
    rows_ref[...] = collect(0)

    first, second, third, last = gram_of(0)
    fill_own(1)

    def reducing(n):
        if n == 0:
            first()
        elif n == 3:
            second()
        elif n == 5:
            third()

    all_gather(1, reducing)
    multiply(1)
    factor = twice(inverse_factor(last()))
    rows_ref[...] = times_transpose(collect(1), factor)

    first, second, third, last = gram_of(1)
    first()
    second()
    third()
    factor = twice(inverse_factor(last()))
    rows_ref[...] = times_transpose(rows_ref[...], factor)
    for t in range(H):
        out_ref[:, t * LANES : (t + 1) * LANES] = rows_ref[pl.ds(t, R, stride=H), :]
    for copy in pending:
        copy.wait_send()


def body(affinity, block_columns, block_counts, inv_degree, panel):
    total_rows = float(affinity.shape[0] * affinity.shape[1] * lax.axis_size("rows") * B)
    dma = pltpu.SemaphoreType.DMA
    out = pl.pallas_call(
        functools.partial(kernel, total_rows),
        out_shape=jax.ShapeDtypeStruct((R, H * LANES), F32),
        in_specs=[
            pl.BlockSpec(memory_space=pltpu.SMEM),
            pl.BlockSpec(memory_space=pltpu.SMEM),
            pl.BlockSpec(memory_space=pl.ANY),
            pl.BlockSpec(memory_space=pltpu.VMEM),
            pl.BlockSpec(memory_space=pltpu.VMEM),
        ],
        out_specs=pl.BlockSpec(memory_space=pltpu.VMEM),
        scratch_shapes=[
            pltpu.VMEM((G, R, S, H * LANES), BF16),
            pltpu.VMEM((G * R, B, S * B), BF16),
            pltpu.VMEM((S * H, LANES), F32),
            pltpu.VMEM((R * H, LANES), F32),
            pltpu.VMEM((R * H, LANES), F32),
            pltpu.VMEM((R * H, LANES), F32),
            pltpu.VMEM((ITERS, NB // 2, B, LANES), BF16),
            pltpu.VMEM((NB + 1, B, LANES), BF16),
            pltpu.VMEM((ITERS, G - 1, R * H, LANES), BF16),
            pltpu.VMEM((ITERS, G, R * H, LANES), BF16),
            pltpu.VMEM((ITERS, G, H, LANES), F32),
            pltpu.VMEM((ITERS, SIDE, H, LANES), F32),
            pltpu.VMEM((ITERS, SIDE, H, LANES), F32),
            dma((G,)),
            dma((ITERS, 60)),
            dma((ITERS, NB // 2)),
            dma((ITERS, G - 1)),
            dma((ITERS, G)),
            dma((ITERS, G - 1)),
            dma((ITERS, G)),
            dma((ITERS, SIDE - 1)),
            dma((ITERS, SIDE)),
            dma((ITERS, SIDE - 1)),
            dma((ITERS, SIDE)),
        ],
        compiler_params=pltpu.CompilerParams(
            collective_id=0, has_side_effects=True, vmem_limit_bytes=40 * 1024 * 1024
        ),
        name="subspace",
    )(
        block_columns[:, :, 0],
        block_counts[:, :, 0],
        affinity[:, :, 0],
        inv_degree[0],
        panel[0],
    )
    return out[None]


def solution(mesh):
    return jax.shard_map(
        body,
        mesh=mesh,
        in_specs=(
            P(None, "rows", "cols", None, None),
            P(None, "rows", "cols", None),
            P(None, "rows", "cols"),
            P("cols", "rows", None),
            P("cols", "rows", None),
        ),
        out_specs=P("cols", "rows", None),
        check_vma=False,
    )
```

profile of v0, /device:TPU:1, one launch (start us, length us, event | category | flops | bytes accessed | tf_op | source)
XLA Modules:
  0.0 72.7 jit_solution(16672428489769037320)
XLA Ops:
  0.0 0.0 copy-start
  0.0 2.2 %copy-done = bf16[8,8,1,8,4096]{4,3,2,1,0:T(8,128)(2,1)S(1)} copy-done((bf16[8,8,1,8,4096]{4,3,2,1,0:T(8,128)(2,1)S(1)}, bf16[8,8,1,8,4096]{4,3,2,1,0:T(8,128)(2,1)}, u32[]{:S(2)}) %copy-start) | copy-done | bytes 4194328
  2.2 0.0 copy-start.1
  2.2 0.9 %copy-done.1 = f32[1,8,4096]{2,1,0:T(8,128)S(1)} copy-done((f32[1,8,4096]{2,1,0:T(8,128)S(1)}, f32[1,8,4096]{2,1,0:T(8,128)}, u32[]{:S(2)}) %copy-start.1) | copy-done | bytes 131096
  3.1 0.0 copy-start.2
  3.1 0.8 %copy-done.2 = s32[8,8,1,8]{3,2,1,0:T(1,128)S(1)} copy-done((s32[8,8,1,8]{3,2,1,0:T(1,128)S(1)}, s32[8,8,1,8]{3,2,1,0:T(1,128)}, u32[]{:S(2)}) %copy-start.2) | copy-done | bytes 2072
  3.9 0.0 copy-start.3
  3.9 0.7 copy-done.3
  4.5 0.0 copy-start.4
  4.5 0.7 copy-done.4
  5.2 66.8 %subspace.1 = f32[8,4096]{1,0:T(8,128)S(1)} custom-call(s32[8,8,8]{2,1,0:T(8,128)S(1)} %bitcast.9, s32[8,8]{1,0:T(8,128)S(1)} %bitcast.10, bf16[8,8,8,4096]{3,2,1,0:T(8,128)(2,1)S(1)} %bitcast.6, f32[8,64]{1,0:T(8,128)S(1)} %bitcast.11, f32[8,4096]{1,0:T(8,128)S(1)} %bitcast.8), custom_call_target="tpu_custom_call" | custom-call | tf_op jit(solution)/shard_map/subspace/pallas_call | solution.py:394
  72.0 0.7 copy.7
Async XLA Ops:
  0.0 2.2 %copy-start = (bf16[8,8,1,8,4096]{4,3,2,1,0:T(8,128)(2,1)S(1)}, bf16[8,8,1,8,4096]{4,3,2,1,0:T(8,128)(2,1)}, u32[]{:S(2)}) copy-start(bf16[8,8,1,8,4096]{4,3,2,1,0:T(8,128)(2,1)} %param.5) | copy-start | bytes 12582916
  2.2 0.9 %copy-start.1 = (f32[1,8,4096]{2,1,0:T(8,128)S(1)}, f32[1,8,4096]{2,1,0:T(8,128)}, u32[]{:S(2)}) copy-start(f32[1,8,4096]{2,1,0:T(8,128)} %param.9) | copy-start | bytes 393220
  3.1 0.8 %copy-start.2 = (s32[8,8,1,8]{3,2,1,0:T(1,128)S(1)}, s32[8,8,1,8]{3,2,1,0:T(1,128)}, u32[]{:S(2)}) copy-start(s32[8,8,1,8]{3,2,1,0:T(1,128)} %param.6) | copy-start | bytes 6148
  3.9 0.7 copy-start.3
  4.5 0.7 copy-start.4
where the time goes:
time: 73.6 us; the launch traced here: 72.7 us
  Pallas kernels  66.8 us (91%)
  local copies, waits for them, and re-layouts  5.88 us (8%)
    pallas_call x1, Pallas kernels, body(): pl.pallas_call(functools.partial(kernel, total_rows), out_shape=jax.Shape...  66.8 us
    unnamed x11, local copies, waits for them, and re-layouts  5.88 us

commit v1 on v0

--- a/solution.py
+++ b/solution.py
@@ -71,11 +71,12 @@
 
 def kernel(
     total_rows,
-    columns_ref, counts_ref, affinity_ref, inverse_ref, panel_ref,
+    columns_hbm, counts_hbm, affinity_ref, inverse_hbm, panel_hbm,
     out_ref,
-    raw, blocks, stage, degree, rows_ref, pack, gathered, table, outgoing, incoming,
-    gram_z, gram_x, gram_y,
-    raw_sem, ag_send, ag_recv, rs_send, rs_recv, gz_send, gz_recv, gx_send, gx_recv, gy_send, gy_recv,
+    columns_ref, counts_ref, inverse_ref, panel_ref,
+    raw, blocks, stage, degree, rows_ref, pack, gathered, table, crossing, crossed, partial,
+    outgoing, incoming, gram_z, gram_p,
+    in_sem, raw_sem, ag_send, ag_recv, core_send, core_recv, rs_send, rs_recv, gz_send, gz_recv, gp_send, gp_recv,
 ):
     mine_r, mine_c = lax.axis_index("rows"), lax.axis_index("cols")
     x, y = mine_r // SIDE, lax.rem(mine_r, SIDE)
@@ -87,11 +88,26 @@
     def col_of(dz, dc):
         return lax.rem(z + dz, SIDE) * 2 + lax.rem(core + dc, 2)
 
-    x_peers = [row_of(d, 0) for d in (1, 2, 3)]
-    y_peers = [row_of(0, d) for d in (1, 2, 3)]
+    x_peers = [row_of(d, 0) for d in (2, 1, 3)]
+    y_peers = [row_of(0, d) for d in (2, 1, 3)]
     order = [(2, 0), (2, 1), (1, 0), (3, 0), (1, 1), (3, 1), (0, 1)]
     z_peers = [col_of(*d) for d in order]
-
+    plane = [row_of(dx, dy) for dx, dy in ((2, 2), (2, 1), (2, 3), (1, 2), (3, 2), (2, 0), (0, 2))]
+    plane += [row_of(dx, dy) for dx in (1, 3) for dy in (1, 3)] + [row_of(*d) for d in ((1, 0), (3, 0), (0, 1), (0, 3))]
+
+    arrivals = [
+        pltpu.make_async_copy(source, target, in_sem.at[n])
+        for n, (source, target) in enumerate(
+            (
+                (panel_hbm, panel_ref),
+                (inverse_hbm, inverse_ref),
+                (columns_hbm, columns_ref),
+                (counts_hbm, counts_ref),
+            )
+        )
+    ]
+    for arrival in arrivals:
+        arrival.start()
     for g in range(G):
         pltpu.make_async_copy(affinity_ref.at[g], raw.at[g], raw_sem.at[g]).start()
 
@@ -100,6 +116,9 @@
         pl.semaphore_signal(barrier, inc=1, device_id={"rows": peer}, device_id_type=MESH)
     for peer in z_peers:
         pl.semaphore_signal(barrier, inc=1, device_id={"cols": peer}, device_id_type=MESH)
+
+    for arrival in arrivals:
+        arrival.wait()
 
     spread = lax.broadcasted_iota(jnp.int32, (H, B), 1) // 2 == lax.broadcasted_iota(jnp.int32, (H, B), 0)
     picked = jnp.concatenate(
@@ -128,9 +147,10 @@
             gathered[it, mine_r * 4 + pair] = pack[pair * B : (pair + 1) * B, :].astype(BF16)
 
     def ag_copy(it, slot, number, peer):
+        both = pl.ds(2 * slot, 2)
         return pltpu.make_async_remote_copy(
-            src_ref=gathered.at[it, slot],
-            dst_ref=gathered.at[it, slot],
+            src_ref=gathered.at[it, both],
+            dst_ref=gathered.at[it, both],
             send_sem=ag_send.at[it, number],
             recv_sem=ag_recv.at[it, slot],
             device_id={"rows": peer},
@@ -147,77 +167,47 @@
 
     def all_gather(it, meanwhile):
         sent = [0]
-        px, nx, py, ny = row_of(1, 0), row_of(-1, 0), row_of(0, 1), row_of(0, -1)
-
-        def slot_of(dx, dy, pair):
-            return row_of(dx, dy) * 4 + pair
-
-        def send(dx, dy, pair, peer):
-            copy = ag_copy(it, slot_of(dx, dy, pair), sent[0], peer)
-            sent[0] += 1
-            copy.start()
-            pending.append(copy)
-
-        def take(dx, dy, pair, *peers):
-            slot = slot_of(dx, dy, pair)
+
+        def slot_of(dx, dy, half):
+            return row_of(dx, dy) * 2 + half
+
+        def send(dx, dy, half, peers):
+            for peer in peers:
+                copy = ag_copy(it, slot_of(dx, dy, half), sent[0], peer)
+                sent[0] += 1
+                copy.start()
+                pending.append(copy)
+
+        def take(dx, dy, half, peers=()):
+            slot = slot_of(dx, dy, half)
             ag_copy(it, slot, 0, mine_r).wait_recv()
-            for peer in peers:
-                send(dx, dy, pair, peer)
-            expand(it, slot)
-
-        for peers_a, peers_b in (((px, nx), (py, ny)), ((py, ny), (px, nx))):
-            for number in range(2):
-                for peer_a, peer_b in zip(peers_a, peers_b):
-                    send(0, 0, number, peer_a)
-                    send(0, 0, 2 + number, peer_b)
+            send(dx, dy, half, peers)
+            for pair in range(2):
+                expand(it, 2 * slot + pair)
+
+        for peer_x, peer_y in zip(x_peers, y_peers):
+            send(0, 0, 0, (peer_x,))
+            send(0, 0, 1, (peer_y,))
+        send(0, 0, 0, y_peers)
+        send(0, 0, 1, x_peers)
         for pair in range(4):
-            expand(it, slot_of(0, 0, pair))
+            expand(it, mine_r * 4 + pair)
         meanwhile(0)
-        take(-1, 0, 0, px, py, ny)
-        take(1, 0, 1, nx, py, ny)
-        take(0, -1, 2, py, px, nx)
-        take(0, 1, 3, ny, px, nx)
-        take(-1, 0, 1, py, ny)
-        take(1, 0, 0, py, ny)
-        take(0, -1, 3, px, nx)
-        take(0, 1, 2, px, nx)
+        for d in (-1, 1):
+            take(d, 0, 0, y_peers)
+            take(0, d, 1, x_peers)
         meanwhile(1)
-        take(0, -1, 0, py)
-        take(0, 1, 1, ny)
-        take(-1, 0, 2, px)
-        take(1, 0, 3, nx)
+        take(2, 0, 0, y_peers)
+        take(0, 2, 1, x_peers)
         meanwhile(2)
-        take(2, 0, 0, py, ny)
-        take(2, 0, 1, py, ny)
-        take(0, 2, 2, px, nx)
-        take(0, 2, 3, px, nx)
+        for d in (-1, 1, 2):
+            take(0, d, 0)
+            take(d, 0, 1)
         meanwhile(3)
-        for d in (-1, 1):
-            take(d, -1, 0, py)
-            take(d, 1, 1, ny)
-            take(-1, d, 2, px)
-            take(1, d, 3, nx)
-        meanwhile(4)
-        take(2, -1, 0, py)
-        take(2, 1, 1, ny)
-        take(-1, 2, 2, px)
-        take(1, 2, 3, nx)
-        meanwhile(5)
-        for d in (0, -1, 1, 2):
-            if d == 0:
-                take(0, -1, 1)
-                take(0, 1, 0)
-                take(-1, 0, 3)
-                take(1, 0, 2)
-            else:
-                take(d, -1, 1)
-                take(d, 1, 0)
-                take(-1, d, 3)
-                take(1, d, 2)
-            take(d, 2, 0)
-            take(d, 2, 1)
-            take(2, d, 2)
-            take(2, d, 3)
+        for d in (-1, 1, 2):
+            for e in (-1, 1, 2):
+                take(e, d, 0)
+                take(d, e, 1)
 
     def arrange(g):
         pltpu.make_async_copy(affinity_ref.at[g], raw.at[g], raw_sem.at[g]).wait()
@@ -245,50 +235,70 @@
         even, odd = o[:H], o[H:]
         return jnp.where(low_h, even, odd) + pltpu.roll(jnp.where(low_h, odd, even), B, 1)
 
-    def rs_copy(it, k, peer):
+    partner = col_of(0, 1)
+    chips = (2, 1, 3, 0)
+
+    def core_copy(it, k):
+        return pltpu.make_async_remote_copy(
+            src_ref=crossing.at[it, k],
+            dst_ref=crossed.at[it, k],
+            send_sem=core_send.at[it, k],
+            recv_sem=core_recv.at[it, k],
+            device_id={"cols": partner},
+            device_id_type=MESH,
+        )
+
+    def rs_copy(it, k, slot, peer):
         return pltpu.make_async_remote_copy(
             src_ref=outgoing.at[it, k],
-            dst_ref=incoming.at[it, mine_c],
+            dst_ref=incoming.at[it, slot],
             send_sem=rs_send.at[it, k],
-            recv_sem=rs_recv.at[it, mine_c],
+            recv_sem=rs_recv.at[it, slot],
             device_id={"cols": peer},
             device_id_type=MESH,
         )
 
     UNROLL = 4
 
+    def products(g, put):
+        def some(step, carry):
+            for j in range(UNROLL):
+                i = step * UNROLL + j
+                put(pl.ds(pl.multiple_of(i * H, H), H), product(g, i))
+            return carry
+
+        lax.fori_loop(0, R // UNROLL, some, 0)
+
     def multiply(it):
-        for k, peer in enumerate(z_peers + [mine_c]):
-            def some(step, carry):
-                for j in range(UNROLL):
-                    i = step * UNROLL + j
-                    term = product(peer, i).astype(BF16)
-                    at = pl.ds(pl.multiple_of(i * H, H), H)
-                    if k < G - 1:
-                        outgoing[it, k, at, :] = term
-                    else:
-                        incoming[it, mine_c, at, :] = term
-                return carry
-
-            lax.fori_loop(0, R // UNROLL, some, 0)
-            if k < G - 1:
-                copy = rs_copy(it, k, peer)
-                copy.start()
-                pending.append(copy)
+        def pass_on(k):
+            core_copy(it, k).wait_recv()
+            outgoing[it, k] = (partial[k] + crossed[it, k].astype(F32)).astype(BF16)
+            copy = rs_copy(it, k, z, col_of(chips[k], 0))
+            copy.start()
+            pending.append(copy)
+
+        for k, dz in enumerate(chips):
+            def put_crossing(at, value, k=k):
+                crossing[it, k, at, :] = value.astype(BF16)
+
+            def put_partial(at, value, k=k):
+                partial[k, at, :] = value
+
+            products(col_of(dz, 1), put_crossing)
+            copy = core_copy(it, k)
+            copy.start()
+            pending.append(copy)
+            products(col_of(dz, 0), put_partial)
+            if k:
+                pass_on(k - 1)
 
     def collect(it):
-        for peer in reversed(z_peers):
-            pltpu.make_async_remote_copy(
-                src_ref=outgoing.at[it, 0],
-                dst_ref=incoming.at[it, peer],
-                send_sem=rs_send.at[it, 0],
-                recv_sem=rs_recv.at[it, peer],
-                device_id={"cols": peer},
-                device_id_type=MESH,
-            ).wait_recv()
-        summed = incoming[it, 0].astype(F32)
-        for c in range(1, G):
-            summed = summed + incoming[it, c].astype(F32)
+        core_copy(it, 3).wait_recv()
+        summed = partial[3] + crossed[it, 3].astype(F32)
+        for k in range(3):
+            slot = lax.rem(z + chips[k], SIDE)
+            rs_copy(it, k, slot, partner).wait_recv()
+            summed = summed + incoming[it, slot].astype(F32)
         return summed * degree[...]
 
     def exchange(it, buffer, send_sem, recv_sem, at, axis, peers, slots):
@@ -320,8 +330,7 @@
 
     def gram_of(it):
         along_z = exchange(it, gram_z, gz_send, gz_recv, mine_c, "cols", z_peers, z_peers)
-        along_x = exchange(it, gram_x, gx_send, gx_recv, x, "rows", x_peers, [p // SIDE for p in x_peers])
-        along_y = exchange(it, gram_y, gy_send, gy_recv, y, "rows", y_peers, [lax.rem(p, SIDE) for p in y_peers])
+        along_plane = exchange(it, gram_p, gp_send, gp_recv, mine_r, "rows", plane, plane)
 
         def first():
             rows = rows_ref[...]
@@ -333,24 +342,20 @@
             along_z[0]()
 
         def second():
-            gram_x[it, x] = along_z[1]()
-            along_x[0]()
-
-        def third():
-            gram_y[it, y] = along_x[1]()
-            along_y[0]()
+            gram_p[it, mine_r] = along_z[1]()
+            along_plane[0]()
 
         def last():
-            total = along_y[1]() * (1.0 / total_rows)
+            total = along_plane[1]() * (1.0 / total_rows)
             return jnp.concatenate([total, pltpu.roll(total, B, 1)], axis=0)
 
-        return first, second, third, last
+        return first, second, last
 
     fill_own(0)
     table[NB] = jnp.zeros((B, LANES), BF16)
     pl.semaphore_wait(barrier, len(x_peers) + len(y_peers) + len(z_peers))
 
-    shares = [(0, 1), (2,), (3,), (4, 5), (6,), (7,)]
+    shares = [(0, 1), (2,), (3, 4), (5, 6, 7)]
 
     def arranging(n):
         for g in shares[n]:
@@ -360,7 +365,7 @@
     multiply(0)
     rows_ref[...] = collect(0)
 
-    first, second, third, last = gram_of(0)
+    first, second, last = gram_of(0)
     fill_own(1)
 
     def reducing(n):
@@ -368,18 +373,15 @@
             first()
         elif n == 3:
             second()
-        elif n == 5:
-            third()
 
     all_gather(1, reducing)
     multiply(1)
     factor = twice(inverse_factor(last()))
     rows_ref[...] = times_transpose(collect(1), factor)
 
-    first, second, third, last = gram_of(1)
+    first, second, last = gram_of(1)
     first()
     second()
-    third()
     factor = twice(inverse_factor(last()))
     rows_ref[...] = times_transpose(rows_ref[...], factor)
     for t in range(H):
@@ -395,14 +397,15 @@
         functools.partial(kernel, total_rows),
         out_shape=jax.ShapeDtypeStruct((R, H * LANES), F32),
         in_specs=[
-            pl.BlockSpec(memory_space=pltpu.SMEM),
-            pl.BlockSpec(memory_space=pltpu.SMEM),
-            pl.BlockSpec(memory_space=pl.ANY),
-            pl.BlockSpec(memory_space=pltpu.VMEM),
-            pl.BlockSpec(memory_space=pltpu.VMEM),
-        ],
+            pl.BlockSpec(memory_space=pltpu.HBM),
+        ]
+        * 5,
         out_specs=pl.BlockSpec(memory_space=pltpu.VMEM),
         scratch_shapes=[
+            pltpu.SMEM((G, R, S), jnp.int32),
+            pltpu.SMEM((G, R), jnp.int32),
+            pltpu.VMEM((R, B), F32),
+            pltpu.VMEM((R, H * LANES), F32),
             pltpu.VMEM((G, R, S, H * LANES), BF16),
             pltpu.VMEM((G * R, B, S * B), BF16),
             pltpu.VMEM((S * H, LANES), F32),
@@ -411,25 +414,28 @@
             pltpu.VMEM((R * H, LANES), F32),
             pltpu.VMEM((ITERS, NB // 2, B, LANES), BF16),
             pltpu.VMEM((NB + 1, B, LANES), BF16),
-            pltpu.VMEM((ITERS, G - 1, R * H, LANES), BF16),
-            pltpu.VMEM((ITERS, G, R * H, LANES), BF16),
+            pltpu.VMEM((ITERS, SIDE, R * H, LANES), BF16),
+            pltpu.VMEM((ITERS, SIDE, R * H, LANES), BF16),
+            pltpu.VMEM((SIDE, R * H, LANES), F32),
+            pltpu.VMEM((ITERS, SIDE - 1, R * H, LANES), BF16),
+            pltpu.VMEM((ITERS, SIDE, R * H, LANES), BF16),
             pltpu.VMEM((ITERS, G, H, LANES), F32),
-            pltpu.VMEM((ITERS, SIDE, H, LANES), F32),
-            pltpu.VMEM((ITERS, SIDE, H, LANES), F32),
+            pltpu.VMEM((ITERS, SIDE * SIDE, H, LANES), F32),
+            dma((4,)),
             dma((G,)),
-            dma((ITERS, 60)),
-            dma((ITERS, NB // 2)),
-            dma((ITERS, G - 1)),
-            dma((ITERS, G)),
-            dma((ITERS, G - 1)),
-            dma((ITERS, G)),
-            dma((ITERS, SIDE - 1)),
+            dma((ITERS, 30)),
+            dma((ITERS, 2 * SIDE * SIDE)),
+            dma((ITERS, SIDE)),
             dma((ITERS, SIDE)),
             dma((ITERS, SIDE - 1)),
             dma((ITERS, SIDE)),
+            dma((ITERS, G - 1)),
+            dma((ITERS, G)),
+            dma((ITERS, SIDE * SIDE - 1)),
+            dma((ITERS, SIDE * SIDE)),
         ],
         compiler_params=pltpu.CompilerParams(
-            collective_id=0, has_side_effects=True, vmem_limit_bytes=40 * 1024 * 1024
+            collective_id=0, has_side_effects=True, vmem_limit_bytes=60 * 1024 * 1024
         ),
         name="subspace",
     )(

time: 73.6 us -> 64.7 us (0.88); the launches traced: 72.7 us -> 64.6 us
  local copies, waits for them, and re-layouts: 5.88 us -> 1.57 us
  Pallas kernels: 66.8 us -> 63 us
    unnamed x11 -> x1, local copies, waits for them, and re-layouts: 5.88 us -> 1.57 us
    pallas_call x1, Pallas kernels: 66.8 us -> 63 us  [body(): pl.pallas_call(functools.partial(kernel, total_rows), out_shape=jax.Shape...]
where the time goes in v1:
time: 64.7 us; the launch traced here: 64.6 us
  Pallas kernels  63 us (97%)
  local copies, waits for them, and re-layouts  1.57 us (2%)
    pallas_call x1, Pallas kernels, body(): pl.pallas_call(functools.partial(kernel, total_rows), out_shape=jax.Shape...  63 us
    unnamed x1, local copies, waits for them, and re-layouts  1.57 us

profile of v1, /device:TPU:1, one launch (start us, length us, event | category | flops | bytes accessed | tf_op | source)
XLA Modules:
  0.0 64.6 jit_solution(18399048743221651224)
XLA Ops:
  0.0 63.0 %subspace.1 = f32[8,4096]{1,0:T(8,128)} custom-call(s32[8,8,8]{2,1,0:T(8,128)} %bitcast.9, s32[8,8]{1,0:T(8,128)} %bitcast.10, bf16[8,8,8,4096]{3,2,1,0:T(8,128)(2,1)} %bitcast.6, f32[8,64]{1,0:T(8,128)} %bitcast.11, f32[8,4096]{1,0:T(8,128)} %bitcast.8), custom_call_target="tpu_custom_call" | custom-call | tf_op jit(solution)/shard_map/subspace/pallas_call | solution.py:396
  63.0 1.6 %copy.7 = f32[1,8,4096]{2,1,0:T(8,128)} copy(f32[1,8,4096]{2,1,0:T(8,128)} %bitcast.7) | data formatting | bytes 262144

commit v2 on v1

--- a/solution.py
+++ b/solution.py
@@ -73,7 +73,7 @@
     total_rows,
     columns_hbm, counts_hbm, affinity_ref, inverse_hbm, panel_hbm,
     out_ref,
-    columns_ref, counts_ref, inverse_ref, panel_ref,
+    columns_ref, counts_ref, index_ref, inverse_ref, panel_ref,
     raw, blocks, stage, degree, rows_ref, pack, gathered, table, crossing, crossed, partial,
     outgoing, incoming, gram_z, gram_p,
     in_sem, raw_sem, ag_send, ag_recv, core_send, core_recv, rs_send, rs_recv, gz_send, gz_recv, gp_send, gp_recv,
@@ -213,6 +213,9 @@
         pltpu.make_async_copy(affinity_ref.at[g], raw.at[g], raw_sem.at[g]).wait()
 
         def one(i, carry):
+            count = counts_ref[g, i]
+            for s in range(S):
+                index_ref[(g * R + i) * S + s] = jnp.where(s < count, columns_ref[g, i, s], NB)
             for t in range(H):
                 stage[pl.ds(t, S, stride=H), :] = raw[g, i, :, t * LANES : (t + 1) * LANES].astype(F32)
             for u in range(S // 2):
@@ -225,15 +228,19 @@
 
         lax.fori_loop(0, R, one, 0)
 
+    def gathered_blocks(g, i):
+        first = (g * R + i) * S
+        return jnp.concatenate([table[index_ref[first + s]] for s in range(S)], axis=0)
+
     def product(g, i):
-        count = counts_ref[g, i]
-        right = []
-        for s in range(S):
-            column = jnp.where(s < count, columns_ref[g, i, s], NB)
-            right.append(table[column])
-        o = jnp.dot(blocks[g * R + i], jnp.concatenate(right, axis=0), preferred_element_type=F32)
-        even, odd = o[:H], o[H:]
-        return jnp.where(low_h, even, odd) + pltpu.roll(jnp.where(low_h, odd, even), B, 1)
+        left = jnp.concatenate([blocks[g * R + i], blocks[g * R + i + 1]], axis=0)
+        right = jnp.concatenate([gathered_blocks(g, i), gathered_blocks(g, i + 1)], axis=1)
+        o = jnp.dot(left, right, preferred_element_type=F32)
+        terms = []
+        for quarter in (o[:B, :LANES], o[B:, LANES:]):
+            even, odd = quarter[:H], quarter[H:]
+            terms.append(jnp.where(low_h, even, odd) + pltpu.roll(jnp.where(low_h, odd, even), B, 1))
+        return jnp.concatenate(terms, axis=0)
 
     partner = col_of(0, 1)
     chips = (2, 1, 3, 0)
@@ -258,16 +265,9 @@
             device_id_type=MESH,
         )
 
-    UNROLL = 4
-
     def products(g, put):
-        def some(step, carry):
-            for j in range(UNROLL):
-                i = step * UNROLL + j
-                put(pl.ds(pl.multiple_of(i * H, H), H), product(g, i))
-            return carry
-
-        lax.fori_loop(0, R // UNROLL, some, 0)
+        for i in range(0, R, 2):
+            put(slice(i * H, i * H + B), product(g, i))
 
     def multiply(it):
         def pass_on(k):
@@ -277,20 +277,32 @@
             copy.start()
             pending.append(copy)
 
-        for k, dz in enumerate(chips):
-            def put_crossing(at, value, k=k):
+        def cross(k):
+            def put(at, value):
                 crossing[it, k, at, :] = value.astype(BF16)
 
-            def put_partial(at, value, k=k):
-                partial[k, at, :] = value
-
-            products(col_of(dz, 1), put_crossing)
+            products(col_of(chips[k], 1), put)
             copy = core_copy(it, k)
             copy.start()
             pending.append(copy)
-            products(col_of(dz, 0), put_partial)
-            if k:
-                pass_on(k - 1)
+
+        def keep(k):
+            def put(at, value):
+                partial[k, at, :] = value
+
+            products(col_of(chips[k], 0), put)
+
+        cross(0)
+        cross(1)
+        keep(0)
+        pass_on(0)
+        cross(2)
+        keep(1)
+        pass_on(1)
+        keep(2)
+        pass_on(2)
+        cross(3)
+        keep(3)
 
     def collect(it):
         core_copy(it, 3).wait_recv()
@@ -368,13 +380,8 @@
     first, second, last = gram_of(0)
     fill_own(1)
 
-    def reducing(n):
-        if n == 0:
-            first()
-        elif n == 3:
-            second()
-
-    all_gather(1, reducing)
+    all_gather(1, lambda n: n == 0 and first())
+    second()
     multiply(1)
     factor = twice(inverse_factor(last()))
     rows_ref[...] = times_transpose(collect(1), factor)
@@ -404,6 +411,7 @@
         scratch_shapes=[
             pltpu.SMEM((G, R, S), jnp.int32),
             pltpu.SMEM((G, R), jnp.int32),
+            pltpu.SMEM((G * R * S,), jnp.int32),
             pltpu.VMEM((R, B), F32),
             pltpu.VMEM((R, H * LANES), F32),
             pltpu.VMEM((G, R, S, H * LANES), BF16),

time: 64.7 us -> 61.9 us (0.957)
  Pallas kernels: 63 us -> 60.2 us
    pallas_call x1, Pallas kernels: 63 us -> 60.2 us  [body(): pl.pallas_call(functools.partial(kernel, total_rows), out_shape=jax.Shape...]
where the time goes in v2:
time: 61.9 us; the launch traced here: 61.8 us
  Pallas kernels  60.2 us (97%)
  local copies, waits for them, and re-layouts  1.57 us (3%)
    pallas_call x1, Pallas kernels, body(): pl.pallas_call(functools.partial(kernel, total_rows), out_shape=jax.Shape...  60.2 us
    unnamed x1, local copies, waits for them, and re-layouts  1.57 us

profile of v2, /device:TPU:1, one launch (start us, length us, event | category | flops | bytes accessed | tf_op | source)
XLA Modules:
  0.0 61.8 jit_solution(6546565782765864188)
XLA Ops:
  0.0 60.2 %subspace.1 = f32[8,4096]{1,0:T(8,128)} custom-call(s32[8,8,8]{2,1,0:T(8,128)} %bitcast.9, s32[8,8]{1,0:T(8,128)} %bitcast.10, bf16[8,8,8,4096]{3,2,1,0:T(8,128)(2,1)} %bitcast.6, f32[8,64]{1,0:T(8,128)} %bitcast.11, f32[8,4096]{1,0:T(8,128)} %bitcast.8), custom_call_target="tpu_custom_call" | custom-call | tf_op jit(solution)/shard_map/subspace/pallas_call | solution.py:403
  60.2 1.6 %copy.7 = f32[1,8,4096]{2,1,0:T(8,128)} copy(f32[1,8,4096]{2,1,0:T(8,128)} %bitcast.7) | data formatting | bytes 262144

commit v3 on v2

--- a/solution.py
+++ b/solution.py
@@ -16,6 +16,7 @@
 H = B // 2
 LANES = 128
 NB = 128
+DISTANCES = (2, 1, 3)
 MESH = pl.DeviceIdType.MESH
 HIGHEST = lax.Precision.HIGHEST
 F32 = jnp.float32
@@ -88,8 +89,8 @@
     def col_of(dz, dc):
         return lax.rem(z + dz, SIDE) * 2 + lax.rem(core + dc, 2)
 
-    x_peers = [row_of(d, 0) for d in (2, 1, 3)]
-    y_peers = [row_of(0, d) for d in (2, 1, 3)]
+    x_peers = [row_of(d, 0) for d in DISTANCES]
+    y_peers = [row_of(0, d) for d in DISTANCES]
     order = [(2, 0), (2, 1), (1, 0), (3, 0), (1, 1), (3, 1), (0, 1)]
     z_peers = [col_of(*d) for d in order]
     plane = [row_of(dx, dy) for dx, dy in ((2, 2), (2, 1), (2, 3), (1, 2), (3, 2), (2, 0), (0, 2))]
@@ -137,27 +138,27 @@
     low_h = low_lanes(H)
     low_b = low_lanes(B)
 
-    def fill_own(it):
-        for pair in range(4):
-            rows = slice(2 * pair * H, 2 * pair * H + B)
-            scaled = rows_ref[rows, :] * degree[rows, :]
-            even, odd = trade(scaled[:H], scaled[H:], low_h)
-            pack[pl.ds(pair * B, H, stride=2), :] = even
-            pack[pl.ds(pair * B + 1, H, stride=2), :] = odd
-            gathered[it, mine_r * 4 + pair] = pack[pair * B : (pair + 1) * B, :].astype(BF16)
-
-    def ag_copy(it, slot, number, peer):
+    def fill_own(it, pair):
+        rows = slice(2 * pair * H, 2 * pair * H + B)
+        scaled = rows_ref[rows, :] * degree[rows, :]
+        even, odd = trade(scaled[:H], scaled[H:], low_h)
+        pack[pl.ds(pair * B, H, stride=2), :] = even
+        pack[pl.ds(pair * B + 1, H, stride=2), :] = odd
+        gathered[it, mine_r * 4 + pair] = pack[pair * B : (pair + 1) * B, :].astype(BF16)
+
+    def ag_copy(it, slot, group, peer):
         both = pl.ds(2 * slot, 2)
         return pltpu.make_async_remote_copy(
             src_ref=gathered.at[it, both],
             dst_ref=gathered.at[it, both],
-            send_sem=ag_send.at[it, number],
-            recv_sem=ag_recv.at[it, slot],
+            send_sem=ag_send.at[it],
+            recv_sem=ag_recv.at[it, group],
             device_id={"rows": peer},
             device_id_type=MESH,
         )
 
-    pending = []
+    def wait_for(ref, sem):
+        pltpu.make_async_copy(ref, ref, sem).wait()
 
     def expand(it, slot):
         pair = gathered[it, slot]
@@ -166,48 +167,55 @@
         table[2 * slot + 1] = jnp.where(low_b, zero, pair)
 
     def all_gather(it, meanwhile):
-        sent = [0]
-
         def slot_of(dx, dy, half):
             return row_of(dx, dy) * 2 + half
 
-        def send(dx, dy, half, peers):
-            for peer in peers:
-                copy = ag_copy(it, slot_of(dx, dy, half), sent[0], peer)
-                sent[0] += 1
-                copy.start()
-                pending.append(copy)
-
-        def take(dx, dy, half, peers=()):
-            slot = slot_of(dx, dy, half)
-            ag_copy(it, slot, 0, mine_r).wait_recv()
-            send(dx, dy, half, peers)
+        def send(dx, dy, half, stage):
+            along_y = (half == 0) == (stage == 1)
+            for n, peer in enumerate(y_peers if along_y else x_peers):
+                ag_copy(it, slot_of(dx, dy, half), 6 * stage + 3 * half + n, peer).start()
+
+        def unpack(dx, dy, half):
             for pair in range(2):
-                expand(it, 2 * slot + pair)
-
-        for peer_x, peer_y in zip(x_peers, y_peers):
-            send(0, 0, 0, (peer_x,))
-            send(0, 0, 1, (peer_y,))
-        send(0, 0, 0, y_peers)
-        send(0, 0, 1, x_peers)
-        for pair in range(4):
-            expand(it, mine_r * 4 + pair)
+                expand(it, 2 * slot_of(dx, dy, half) + pair)
+
+        def take(n, half):
+            d = -DISTANCES[n]
+            at = (d, 0) if half == 0 else (0, d)
+            wait_for(gathered.at[it, pl.ds(0, 2)], ag_recv.at[it, 3 * half + n])
+            send(*at, half, 1)
+            return at
+
+        def take_all(n, half):
+            d = -DISTANCES[n]
+            wait_for(gathered.at[it, pl.ds(0, 2 * SIDE)], ag_recv.at[it, 6 + 3 * half + n])
+            for e in range(SIDE):
+                at = (e, d) if half == 0 else (d, e)
+                unpack(*at, half)
+
+        send(0, 0, 0, 1)
+        send(0, 0, 1, 1)
+        for half in range(2):
+            unpack(0, 0, half)
         meanwhile(0)
-        for d in (-1, 1):
-            take(d, 0, 0, y_peers)
-            take(0, d, 1, x_peers)
+        for n in (1, 2):
+            for half in range(2):
+                at = take(n, half)
+                unpack(*at, half)
         meanwhile(1)
-        take(2, 0, 0, y_peers)
-        take(0, 2, 1, x_peers)
+        for half in range(2):
+            at = take(0, half)
+            unpack(*at, half)
         meanwhile(2)
-        for d in (-1, 1, 2):
-            take(0, d, 0)
-            take(d, 0, 1)
+        for n in (1, 2, 0):
+            for half in range(2):
+                take_all(n, half)
         meanwhile(3)
-        for d in (-1, 1, 2):
-            for e in (-1, 1, 2):
-                take(e, d, 0)
-                take(d, e, 1)
+        wait_for(gathered.at[it, pl.ds(0, 60)], ag_send.at[it])
+
+    def send_own(it, half):
+        for n, peer in enumerate(y_peers if half else x_peers):
+            ag_copy(it, mine_r * 2 + half, 3 * half + n, peer).start()
 
     def arrange(g):
         pltpu.make_async_copy(affinity_ref.at[g], raw.at[g], raw_sem.at[g]).wait()
@@ -249,7 +257,7 @@
         return pltpu.make_async_remote_copy(
             src_ref=crossing.at[it, k],
             dst_ref=crossed.at[it, k],
-            send_sem=core_send.at[it, k],
+            send_sem=core_send.at[it],
             recv_sem=core_recv.at[it, k],
             device_id={"cols": partner},
             device_id_type=MESH,
@@ -259,8 +267,8 @@
         return pltpu.make_async_remote_copy(
             src_ref=outgoing.at[it, k],
             dst_ref=incoming.at[it, slot],
-            send_sem=rs_send.at[it, k],
-            recv_sem=rs_recv.at[it, slot],
+            send_sem=rs_send.at[it],
+            recv_sem=rs_recv.at[it],
             device_id={"cols": peer},
             device_id_type=MESH,
         )
@@ -273,18 +281,14 @@
         def pass_on(k):
             core_copy(it, k).wait_recv()
             outgoing[it, k] = (partial[k] + crossed[it, k].astype(F32)).astype(BF16)
-            copy = rs_copy(it, k, z, col_of(chips[k], 0))
-            copy.start()
-            pending.append(copy)
+            rs_copy(it, k, z, col_of(chips[k], 0)).start()
 
         def cross(k):
             def put(at, value):
                 crossing[it, k, at, :] = value.astype(BF16)
 
             products(col_of(chips[k], 1), put)
-            copy = core_copy(it, k)
-            copy.start()
-            pending.append(copy)
+            core_copy(it, k).start()
 
         def keep(k):
             def put(at, value):
@@ -304,35 +308,35 @@
         cross(3)
         keep(3)
 
-    def collect(it):
+    def await_sums(it):
         core_copy(it, 3).wait_recv()
-        summed = partial[3] + crossed[it, 3].astype(F32)
+        wait_for(crossing.at[it], core_send.at[it])
+        wait_for(outgoing.at[it], rs_send.at[it])
+        wait_for(outgoing.at[it], rs_recv.at[it])
+
+    def collect(it, rows):
+        summed = partial[3, rows, :] + crossed[it, 3, rows, :].astype(F32)
         for k in range(3):
-            slot = lax.rem(z + chips[k], SIDE)
-            rs_copy(it, k, slot, partner).wait_recv()
-            summed = summed + incoming[it, slot].astype(F32)
-        return summed * degree[...]
-
-    def exchange(it, buffer, send_sem, recv_sem, at, axis, peers, slots):
-        def copy(n, slot):
-            return pltpu.make_async_remote_copy(
-                src_ref=buffer.at[it, at],
-                dst_ref=buffer.at[it, slot],
-                send_sem=send_sem.at[it, n],
-                recv_sem=recv_sem.at[it, slot],
-                device_id={axis: peers[n]},
-                device_id_type=MESH,
-            )
+            summed = summed + incoming[it, lax.rem(z + chips[k], SIDE), rows, :].astype(F32)
+        return summed * degree[rows, :]
+
+    def exchange(it, buffer, send_sem, recv_sem, at, axis, peers):
+        others = buffer.at[it, pl.ds(0, len(peers))]
 
         def start():
-            for n in range(len(peers)):
-                c = copy(n, at)
-                c.start()
-                pending.append(c)
+            for peer in peers:
+                pltpu.make_async_remote_copy(
+                    src_ref=buffer.at[it, at],
+                    dst_ref=buffer.at[it, at],
+                    send_sem=send_sem.at[it],
+                    recv_sem=recv_sem.at[it],
+                    device_id={axis: peer},
+                    device_id_type=MESH,
+                ).start()
 
         def finish():
-            for n in range(len(peers)):
-                copy(n, slots[n]).wait_recv()
+            wait_for(others, recv_sem.at[it])
+            wait_for(others, send_sem.at[it])
             total = buffer[it, 0]
             for n in range(1, len(peers) + 1):
                 total = total + buffer[it, n]
@@ -341,8 +345,8 @@
         return start, finish
 
     def gram_of(it):
-        along_z = exchange(it, gram_z, gz_send, gz_recv, mine_c, "cols", z_peers, z_peers)
-        along_plane = exchange(it, gram_p, gp_send, gp_recv, mine_r, "rows", plane, plane)
+        along_z = exchange(it, gram_z, gz_send, gz_recv, mine_c, "cols", z_peers)
+        along_plane = exchange(it, gram_p, gp_send, gp_recv, mine_r, "rows", plane)
 
         def first():
             rows = rows_ref[...]
@@ -363,9 +367,12 @@
 
         return first, second, last
 
-    fill_own(0)
+    for pair in range(4):
+        fill_own(0, pair)
     table[NB] = jnp.zeros((B, LANES), BF16)
     pl.semaphore_wait(barrier, len(x_peers) + len(y_peers) + len(z_peers))
+    for half in range(2):
+        send_own(0, half)
 
     shares = [(0, 1), (2,), (3, 4), (5, 6, 7)]
 
@@ -375,16 +382,21 @@
 
     all_gather(0, arranging)
     multiply(0)
-    rows_ref[...] = collect(0)
-
+
+    await_sums(0)
+    for half in range(2):
+        for pair in (2 * half, 2 * half + 1):
+            rows = slice(2 * pair * H, 2 * pair * H + B)
+            rows_ref[rows, :] = collect(0, rows)
+            fill_own(1, pair)
+        send_own(1, half)
     first, second, last = gram_of(0)
-    fill_own(1)
-
     all_gather(1, lambda n: n == 0 and first())
     second()
     multiply(1)
     factor = twice(inverse_factor(last()))
-    rows_ref[...] = times_transpose(collect(1), factor)
+    await_sums(1)
+    rows_ref[...] = times_transpose(collect(1, slice(None)), factor)
 
     first, second, last = gram_of(1)
     first()
@@ -393,8 +405,6 @@
     rows_ref[...] = times_transpose(rows_ref[...], factor)
     for t in range(H):
         out_ref[:, t * LANES : (t + 1) * LANES] = rows_ref[pl.ds(t, R, stride=H), :]
-    for copy in pending:
-        copy.wait_send()
 
 
 def body(affinity, block_columns, block_counts, inv_degree, panel):
@@ -431,16 +441,16 @@
             pltpu.VMEM((ITERS, SIDE * SIDE, H, LANES), F32),
             dma((4,)),
             dma((G,)),
-            dma((ITERS, 30)),
-            dma((ITERS, 2 * SIDE * SIDE)),
+            dma((ITERS,)),
+            dma((ITERS, 12)),
+            dma((ITERS,)),
             dma((ITERS, SIDE)),
-            dma((ITERS, SIDE)),
-            dma((ITERS, SIDE - 1)),
-            dma((ITERS, SIDE)),
-            dma((ITERS, G - 1)),
-            dma((ITERS, G)),
-            dma((ITERS, SIDE * SIDE - 1)),
-            dma((ITERS, SIDE * SIDE)),
+            dma((ITERS,)),
+            dma((ITERS,)),
+            dma((ITERS,)),
+            dma((ITERS,)),
+            dma((ITERS,)),
+            dma((ITERS,)),
         ],
         compiler_params=pltpu.CompilerParams(
             collective_id=0, has_side_effects=True, vmem_limit_bytes=60 * 1024 * 1024

time: 61.9 us -> 61.2 us (0.989)
  Pallas kernels: 60.2 us -> 59.5 us
    pallas_call x1, Pallas kernels: 60.2 us -> 59.5 us  [body(): pl.pallas_call(functools.partial(kernel, total_rows), out_shape=jax.Shape...]
where the time goes in v3:
time: 61.2 us; the launch traced here: 61 us
  Pallas kernels  59.5 us (97%)
  local copies, waits for them, and re-layouts  1.57 us (3%)
    pallas_call x1, Pallas kernels, body(): pl.pallas_call(functools.partial(kernel, total_rows), out_shape=jax.Shape...  59.5 us
    unnamed x1, local copies, waits for them, and re-layouts  1.57 us

profile of v3, /device:TPU:1, one launch (start us, length us, event | category | flops | bytes accessed | tf_op | source)
XLA Modules:
  0.0 61.0 jit_solution(3050169147932685374)
XLA Ops:
  0.0 59.5 %subspace.1 = f32[8,4096]{1,0:T(8,128)} custom-call(s32[8,8,8]{2,1,0:T(8,128)} %bitcast.9, s32[8,8]{1,0:T(8,128)} %bitcast.10, bf16[8,8,8,4096]{3,2,1,0:T(8,128)(2,1)} %bitcast.6, f32[8,64]{1,0:T(8,128)} %bitcast.11, f32[8,4096]{1,0:T(8,128)} %bitcast.8), custom_call_target="tpu_custom_call" | custom-call | tf_op jit(solution)/shard_map/subspace/pallas_call | solution.py:413
  59.5 1.6 %copy.7 = f32[1,8,4096]{2,1,0:T(8,128)} copy(f32[1,8,4096]{2,1,0:T(8,128)} %bitcast.7) | data formatting | bytes 262144

commit v4 on v3

--- a/solution.py
+++ b/solution.py
@@ -16,6 +16,7 @@
 H = B // 2
 LANES = 128
 NB = 128
+PANEL = 8
 DISTANCES = (2, 1, 3)
 MESH = pl.DeviceIdType.MESH
 HIGHEST = lax.Precision.HIGHEST
@@ -37,21 +38,23 @@
     lane = lax.broadcasted_iota(jnp.int32, (B, LANES), 1)
     m = jnp.where(lane < B, gram, jnp.where(lane - B == row, 1.0, 0.0).astype(F32))
     done = []
-    for block in range(B // 8):
-        height = B - 8 * block
+    for start in range(0, B, PANEL):
+        offset = start % 8
+        height = B - start + offset
         rows = lax.broadcasted_iota(jnp.int32, (height, LANES), 0)
         columns = [
-            jnp.broadcast_to(m[:, 8 * block + j : 8 * block + j + 1], (height, LANES))
-            for j in range(8)
+            jnp.broadcast_to(m[:, start + j : start + j + 1], (height, LANES)) for j in range(PANEL)
         ]
-        for j in range(8):
-            ratio = columns[j] * (1.0 / columns[j][j : j + 1, :])
-            ratio = jnp.where(rows > j, ratio, 0.0)
-            for later in range(j + 1, 8):
-                columns[later] = columns[later] - ratio * columns[later][j : j + 1, :]
-            m = m - ratio * m[j : j + 1, :]
-        done.append(m[:8])
-        m = m[8:]
+        for j in range(PANEL):
+            at = offset + j
+            ratio = columns[j] * (1.0 / columns[j][at : at + 1, :])
+            ratio = jnp.where(rows > at, ratio, 0.0)
+            for later in range(j + 1, PANEL):
+                columns[later] = columns[later] - ratio * columns[later][at : at + 1, :]
+            m = m - ratio * m[at : at + 1, :]
+        if offset + PANEL == 8:
+            done.append(m[:8])
+            m = m[8:]
     m = jnp.concatenate(done, axis=0)
     pivots = jnp.sum(jnp.where(lane == row, m, 0.0), axis=1, keepdims=True)
     return m * lax.rsqrt(pivots)
@@ -391,8 +394,8 @@
             fill_own(1, pair)
         send_own(1, half)
     first, second, last = gram_of(0)
-    all_gather(1, lambda n: n == 0 and first())
-    second()
+    reducing = {0: first, 3: second}
+    all_gather(1, lambda n: n in reducing and reducing[n]())
     multiply(1)
     factor = twice(inverse_factor(last()))
     await_sums(1)
@@ -453,15 +456,14 @@
             dma((ITERS,)),
         ],
         compiler_params=pltpu.CompilerParams(
-            collective_id=0, has_side_effects=True, vmem_limit_bytes=60 * 1024 * 1024
+            collective_id=0, has_side_effects=True, vmem_limit_bytes=40 * 1024 * 1024
         ),
         name="subspace",
     )(
-        block_columns[:, :, 0],
-        block_counts[:, :, 0],
-        affinity[:, :, 0],
-        inv_degree[0],
-        panel[0],
+        *(
+            pltpu.with_memory_space_constraint(argument, pltpu.HBM)
+            for argument in (block_columns[:, :, 0], block_counts[:, :, 0], affinity[:, :, 0], inv_degree[0], panel[0])
+        )
     )
     return out[None]
 

time: 61.2 us -> 59.6 us (0.974)
  local copies, waits for them, and re-layouts: 1.57 us -> 0.66 us
  Pallas kernels: 59.5 us -> 58.8 us
    unnamed x1, local copies, waits for them, and re-layouts: 1.57 us -> 0.66 us
    pallas_call x1, Pallas kernels: 59.5 us -> 58.8 us  [body(): pl.pallas_call(functools.partial(kernel, total_rows), out_shape=jax.Shape...]
where the time goes in v4:
time: 59.6 us; the launch traced here: 59.5 us
  Pallas kernels  58.8 us (99%)
  local copies, waits for them, and re-layouts  0.66 us (1%)
    pallas_call x1, Pallas kernels, body(): pl.pallas_call(functools.partial(kernel, total_rows), out_shape=jax.Shape...  58.8 us

profile of v4, /device:TPU:1, one launch (start us, length us, event | category | flops | bytes accessed | tf_op | source)
XLA Modules:
  0.0 59.5 jit_solution(2922100064478470194)
XLA Ops:
  0.0 58.8 %subspace.1 = f32[8,4096]{1,0:T(8,128)S(1)} custom-call(s32[8,8,8]{2,1,0:T(8,128)} %bitcast.9, s32[8,8]{1,0:T(8,128)} %bitcast.10, bf16[8,8,8,4096]{3,2,1,0:T(8,128)(2,1)} %bitcast.7, f32[8,64]{1,0:T(8,128)} %bitcast.11, f32[8,4096]{1,0:T(8,128)} %bitcast.8), custom_call_target="tpu_custom_call" | custom-call | tf_op jit(solution)/shard_map/subspace/pallas_call | solution.py:416
  58.8 0.7 %copy.7 = f32[1,8,4096]{2,1,0:T(8,128)} copy(f32[1,8,4096]{2,1,0:T(8,128)S(1)} %bitcast.6) | data formatting | bytes 262144

commit v5 on v4

--- a/solution.py
+++ b/solution.py
@@ -228,10 +228,10 @@
             for s in range(S):
                 index_ref[(g * R + i) * S + s] = jnp.where(s < count, columns_ref[g, i, s], NB)
             for t in range(H):
-                stage[pl.ds(t, S, stride=H), :] = raw[g, i, :, t * LANES : (t + 1) * LANES].astype(F32)
+                stage[t * S : (t + 1) * S, :] = raw[g, i, :, t * LANES : (t + 1) * LANES].astype(F32)
             for u in range(S // 2):
                 upper, lower = trade(
-                    stage[2 * u * H : (2 * u + 1) * H, :], stage[(2 * u + 1) * H : (2 * u + 2) * H, :], low_h
+                    stage[pl.ds(2 * u, H, stride=S), :], stage[pl.ds(2 * u + 1, H, stride=S), :], low_h
                 )
                 blocks[g * R + i, 0:H, u * LANES : (u + 1) * LANES] = upper.astype(BF16)
                 blocks[g * R + i, H:B, u * LANES : (u + 1) * LANES] = lower.astype(BF16)
@@ -256,66 +256,82 @@
     partner = col_of(0, 1)
     chips = (2, 1, 3, 0)
 
-    def core_copy(it, k):
+    def half_rows(half):
+        return slice(half * R * H // 2, (half + 1) * R * H // 2)
+
+    def core_copy(it, k, half):
+        rows = pl.ds(half * R * H // 2, R * H // 2)
         return pltpu.make_async_remote_copy(
-            src_ref=crossing.at[it, k],
-            dst_ref=crossed.at[it, k],
+            src_ref=crossing.at[it, k, rows],
+            dst_ref=crossed.at[it, k, rows],
             send_sem=core_send.at[it],
-            recv_sem=core_recv.at[it, k],
+            recv_sem=core_recv.at[it, SIDE * half + k],
             device_id={"cols": partner},
             device_id_type=MESH,
         )
 
-    def rs_copy(it, k, slot, peer):
+    def rs_copy(it, k, half, peer):
+        rows = pl.ds(half * R * H // 2, R * H // 2)
         return pltpu.make_async_remote_copy(
-            src_ref=outgoing.at[it, k],
-            dst_ref=incoming.at[it, slot],
+            src_ref=outgoing.at[it, k, rows],
+            dst_ref=incoming.at[it, z, rows],
             send_sem=rs_send.at[it],
-            recv_sem=rs_recv.at[it],
+            recv_sem=rs_recv.at[it, half],
             device_id={"cols": peer},
             device_id_type=MESH,
         )
 
-    def products(g, put):
-        for i in range(0, R, 2):
+    def products(g, half, put):
+        for i in range(half * R // 2, (half + 1) * R // 2, 2):
             put(slice(i * H, i * H + B), product(g, i))
 
     def multiply(it):
-        def pass_on(k):
-            core_copy(it, k).wait_recv()
-            outgoing[it, k] = (partial[k] + crossed[it, k].astype(F32)).astype(BF16)
-            rs_copy(it, k, z, col_of(chips[k], 0)).start()
-
-        def cross(k):
+        def cross(k, half):
             def put(at, value):
                 crossing[it, k, at, :] = value.astype(BF16)
 
-            products(col_of(chips[k], 1), put)
-            core_copy(it, k).start()
-
-        def keep(k):
+            products(col_of(chips[k], 1), half, put)
+
+        def keep(k, half):
             def put(at, value):
                 partial[k, at, :] = value
 
-            products(col_of(chips[k], 0), put)
-
-        cross(0)
-        cross(1)
-        keep(0)
-        pass_on(0)
-        cross(2)
-        keep(1)
-        pass_on(1)
-        keep(2)
-        pass_on(2)
-        cross(3)
-        keep(3)
-
-    def await_sums(it):
-        core_copy(it, 3).wait_recv()
-        wait_for(crossing.at[it], core_send.at[it])
-        wait_for(outgoing.at[it], rs_send.at[it])
-        wait_for(outgoing.at[it], rs_recv.at[it])
+            products(col_of(chips[k], 0), half, put)
+
+        def pass_on(k, half):
+            core_copy(it, k, half).wait_recv()
+            rows = half_rows(half)
+            outgoing[it, k, rows, :] = (partial[k, rows, :] + crossed[it, k, rows, :].astype(F32)).astype(BF16)
+            rs_copy(it, k, half, col_of(chips[k], 0)).start()
+
+        for half in range(2):
+            cross(0, half)
+            cross(1, half)
+            core_copy(it, 0, half).start()
+            core_copy(it, 1, half).start()
+            if half == 1:
+                pass_on(2, 0)
+            cross(2, half)
+            keep(0, half)
+            core_copy(it, 2, half).start()
+            keep(1, half)
+            keep(2, half)
+            pass_on(0, half)
+            pass_on(1, half)
+        cross(3, 0)
+        cross(3, 1)
+        core_copy(it, 3, 0).start()
+        core_copy(it, 3, 1).start()
+        pass_on(2, 1)
+        keep(3, 0)
+        keep(3, 1)
+
+    def await_sums(it, half):
+        core_copy(it, 3, half).wait_recv()
+        wait_for(gathered.at[it, pl.ds(0, 6)], rs_recv.at[it, half])
+        if half == 1:
+            wait_for(crossing.at[it], core_send.at[it])
+            wait_for(outgoing.at[it], rs_send.at[it])
 
     def collect(it, rows):
         summed = partial[3, rows, :] + crossed[it, 3, rows, :].astype(F32)
@@ -386,8 +402,8 @@
     all_gather(0, arranging)
     multiply(0)
 
-    await_sums(0)
     for half in range(2):
+        await_sums(0, half)
         for pair in (2 * half, 2 * half + 1):
             rows = slice(2 * pair * H, 2 * pair * H + B)
             rows_ref[rows, :] = collect(0, rows)
@@ -398,7 +414,8 @@
     all_gather(1, lambda n: n in reducing and reducing[n]())
     multiply(1)
     factor = twice(inverse_factor(last()))
-    await_sums(1)
+    for half in range(2):
+        await_sums(1, half)
     rows_ref[...] = times_transpose(collect(1, slice(None)), factor)
 
     first, second, last = gram_of(1)
@@ -447,9 +464,9 @@
             dma((ITERS,)),
             dma((ITERS, 12)),
             dma((ITERS,)),
-            dma((ITERS, SIDE)),
-            dma((ITERS,)),
-            dma((ITERS,)),
+            dma((ITERS, 2 * SIDE)),
+            dma((ITERS,)),
+            dma((ITERS, 2)),
             dma((ITERS,)),
             dma((ITERS,)),
             dma((ITERS,)),

time: 59.6 us -> 58.1 us (0.975)
  Pallas kernels: 58.8 us -> 57.3 us
    pallas_call x1, Pallas kernels: 58.8 us -> 57.3 us  [body(): pl.pallas_call(functools.partial(kernel, total_rows), out_shape=jax.Shape...]
where the time goes in v5:
time: 58.1 us; the launch traced here: 58 us
  Pallas kernels  57.3 us (99%)
  local copies, waits for them, and re-layouts  0.66 us (1%)
    pallas_call x1, Pallas kernels, body(): pl.pallas_call(functools.partial(kernel, total_rows), out_shape=jax.Shape...  57.3 us

profile of v5, /device:TPU:1, one launch (start us, length us, event | category | flops | bytes accessed | tf_op | source)
XLA Modules:
  0.0 58.0 jit_solution(3863501751887681452)
XLA Ops:
  0.0 57.3 %subspace.1 = f32[8,4096]{1,0:T(8,128)S(1)} custom-call(s32[8,8,8]{2,1,0:T(8,128)} %bitcast.9, s32[8,8]{1,0:T(8,128)} %bitcast.10, bf16[8,8,8,4096]{3,2,1,0:T(8,128)(2,1)} %bitcast.7, f32[8,64]{1,0:T(8,128)} %bitcast.11, f32[8,4096]{1,0:T(8,128)} %bitcast.8), custom_call_target="tpu_custom_call" | custom-call | tf_op jit(solution)/shard_map/subspace/pallas_call | solution.py:433
  57.3 0.7 %copy.7 = f32[1,8,4096]{2,1,0:T(8,128)} copy(f32[1,8,4096]{2,1,0:T(8,128)S(1)} %bitcast.6) | data formatting | bytes 262144

commit v6 on v5

--- a/solution.py
+++ b/solution.py
@@ -393,7 +393,7 @@
     for half in range(2):
         send_own(0, half)
 
-    shares = [(0, 1), (2,), (3, 4), (5, 6, 7)]
+    shares = [(0, 1, 2), (3,), (4, 5, 6, 7), ()]
 
     def arranging(n):
         for g in shares[n]:

time: 58.1 us -> 55.6 us (0.957)
  Pallas kernels: 57.3 us -> 54.8 us
    pallas_call x1, Pallas kernels: 57.3 us -> 54.8 us  [body(): pl.pallas_call(functools.partial(kernel, total_rows), out_shape=jax.Shape...]
where the time goes in v6:
time: 55.6 us; the launch traced here: 55.5 us
  Pallas kernels  54.8 us (99%)
  local copies, waits for them, and re-layouts  0.66 us (1%)
    pallas_call x1, Pallas kernels, body(): pl.pallas_call(functools.partial(kernel, total_rows), out_shape=jax.Shape...  54.8 us

profile of v6, /device:TPU:1, one launch (start us, length us, event | category | flops | bytes accessed | tf_op | source)
XLA Modules:
  0.0 55.5 jit_solution(4949564686430279555)
XLA Ops:
  0.0 54.8 %subspace.1 = f32[8,4096]{1,0:T(8,128)S(1)} custom-call(s32[8,8,8]{2,1,0:T(8,128)} %bitcast.9, s32[8,8]{1,0:T(8,128)} %bitcast.10, bf16[8,8,8,4096]{3,2,1,0:T(8,128)(2,1)} %bitcast.7, f32[8,64]{1,0:T(8,128)} %bitcast.11, f32[8,4096]{1,0:T(8,128)} %bitcast.8), custom_call_target="tpu_custom_call" | custom-call | tf_op jit(solution)/shard_map/subspace/pallas_call | solution.py:433
  54.8 0.7 %copy.7 = f32[1,8,4096]{2,1,0:T(8,128)} copy(f32[1,8,4096]{2,1,0:T(8,128)S(1)} %bitcast.6) | data formatting | bytes 262144

commit v7 on v6

--- a/solution.py
+++ b/solution.py
@@ -393,7 +393,7 @@
     for half in range(2):
         send_own(0, half)
 
-    shares = [(0, 1, 2), (3,), (4, 5, 6, 7), ()]
+    shares = [(0, 1), (2, 3), (4, 5, 6, 7), ()]
 
     def arranging(n):
         for g in shares[n]:

time: 55.6 us -> 56 us (level)
  no operation moved by 1% of the time
where the time goes in v7:
time: 56 us; the launch traced here: 55.9 us
  Pallas kernels  55.2 us (99%)
  local copies, waits for them, and re-layouts  0.66 us (1%)
    pallas_call x1, Pallas kernels, body(): pl.pallas_call(functools.partial(kernel, total_rows), out_shape=jax.Shape...  55.2 us

profile of v7, /device:TPU:1, one launch (start us, length us, event | category | flops | bytes accessed | tf_op | source)
XLA Modules:
  0.0 55.9 jit_solution(3636272718007593562)
XLA Ops:
  0.0 55.2 %subspace.1 = f32[8,4096]{1,0:T(8,128)S(1)} custom-call(s32[8,8,8]{2,1,0:T(8,128)} %bitcast.9, s32[8,8]{1,0:T(8,128)} %bitcast.10, bf16[8,8,8,4096]{3,2,1,0:T(8,128)(2,1)} %bitcast.7, f32[8,64]{1,0:T(8,128)} %bitcast.11, f32[8,4096]{1,0:T(8,128)} %bitcast.8), custom_call_target="tpu_custom_call" | custom-call | tf_op jit(solution)/shard_map/subspace/pallas_call | solution.py:433
  55.2 0.7 %copy.7 = f32[1,8,4096]{2,1,0:T(8,128)} copy(f32[1,8,4096]{2,1,0:T(8,128)S(1)} %bitcast.6) | data formatting | bytes 262144
